TPU v7x, 32 devices: a whole 2x2x4 slice. The times are simulated.
32 devices in a mesh: dp: 8 (over z, y), fsdp: 4 (over x, core).
Axes of the slice: x: 2, y: 2, z: 4, core: 2. Of those that a mesh axis runs over, the one named last changes fastest.
Arguments:
- hidden_in: float32 [8192, 768], P(('dp', 'fsdp')), may hold values from -6 to 6
- cotangent: float32 [8192, 768], P(('dp', 'fsdp')), may hold values from -6 to 6
- seq_ids: int32 [8192], P(('dp', 'fsdp')), may hold values from -1 to 8191, as said below
- norm_gain: bfloat16 [768], P(('dp', 'fsdp')), may hold values from 0.5 to 1.5
- in_weight: bfloat16 [768, 3352], P(('dp', 'fsdp')), may hold values from -0.21875 to 0.21875
- conv_weight: bfloat16 [4, 1792], P(None, ('dp', 'fsdp')), may hold values from -3 to 3
- conv_bias: bfloat16 [1792], P(('dp', 'fsdp')), may hold values from -3 to 3
- out_gain: bfloat16 [1536], P(('dp', 'fsdp')), may hold values from 0.5 to 1.5
- out_weight: bfloat16 [1536, 768], P(('dp', 'fsdp')), may hold values from -0.15625 to 0.15625
- decay_log: float32 [24], replicated, may hold values from 0 to 2.77
- skip_gain: float32 [24], replicated, may hold values from 0.5 to 1.5
- step_bias: float32 [24], replicated, may hold values from -4.6 to -0.5
Outputs:
- block_out: float32 [8192, 768], P(('dp', 'fsdp'))
- grad_hidden: float32 [8192, 768], P(('dp', 'fsdp'))
- grad_norm_gain: float32 [768], P(('dp', 'fsdp'))
- grad_in_weight: float32 [768, 3352], P(('dp', 'fsdp'))
- grad_conv_weight: float32 [4, 1792], P(None, ('dp', 'fsdp'))
- grad_conv_bias: float32 [1792], P(('dp', 'fsdp'))
- grad_out_gain: float32 [1536], P(('dp', 'fsdp'))
- grad_out_weight: float32 [1536, 768], P(('dp', 'fsdp'))
- grad_decay_log: float32 [24], replicated
- grad_skip_gain: float32 [24], replicated
- grad_step_bias: float32 [24], replicated
Inputs may be any that keep to these rules, and one draw needn't show every extreme that they name: `seq_ids`: in each aligned block of 256 slots the live slots come first and the rest hold -1; a sequence fills consecutive slots inside one block and its numbers rise along the slots; a sequence has at most 256 tokens, and some sequence has exactly 256; the first block has no empty slot.
All inputs are finite; a program needn't handle non-finite values.
Results may differ from a plain program's by a relative error of at most 0.015.
Values may be sent and summed in bfloat16 or wider, within the bound.
A program may use at most 128 MiB of HBM per device.

v0:
```python
from functools import partial

import jax
import jax.numpy as jnp
from jax import lax
from jax.sharding import PartitionSpec as P

NS = 128
HD = 64
NH = 24
KC = 4
SPAN = 128
DI = 1536
CONV = 1792


EPS = 1e-05


def norm_input(hidden, gain):
    scale = lax.rsqrt(jnp.mean(hidden * hidden, axis=-1, keepdims=True) + EPS)
    return hidden * scale * gain[None, :]


def mixer(
    projected, conv_kernel, conv_shift, out_scale, decay_log, skip_gain, step_bias, seq_index
):
    length = projected.shape[0]
    gate_part = projected[:, :DI]
    conv_in = projected[:, DI : DI + CONV]
    step_raw = projected[:, DI + CONV :]
    live_rows = (seq_index >= 0).astype(jnp.float32)
    summed = conv_shift[None, :] + conv_in * conv_kernel[KC - 1][None, :]
    for offset in range(1, KC):
        earlier = jnp.concatenate(
            [jnp.zeros((offset, CONV), jnp.float32), conv_in[: length - offset]], axis=0
        )
        matched = (seq_index[offset:] == seq_index[: length - offset]).astype(jnp.float32)
        same_seq = jnp.concatenate([jnp.zeros((offset,), jnp.float32), matched], axis=0)
        summed = summed + earlier * same_seq[:, None] * conv_kernel[KC - 1 - offset][None, :]
    activated = jax.nn.silu(summed)
    values = activated[:, :DI]
    in_state = activated[:, DI : DI + NS]
    out_state = activated[:, DI + NS :]
    step_size = jax.nn.softplus(step_raw + step_bias[None, :])
    log_decay = step_size * (-jnp.exp(decay_log))[None, :]
    blocks = length // SPAN
    scaled = (values.reshape(length, NH, HD) * step_size[:, :, None]).reshape(blocks, SPAN, NH, HD)
    keys_in = in_state.reshape(blocks, SPAN, NS)
    query_out = out_state.reshape(blocks, SPAN, NS)
    seq_blocks = seq_index.reshape(blocks, SPAN)
    running = jnp.cumsum(log_decay.reshape(blocks, SPAN, NH), axis=1).transpose(0, 2, 1)
    row_pos = lax.broadcasted_iota(jnp.int32, (SPAN, SPAN), 0)
    col_pos = lax.broadcasted_iota(jnp.int32, (SPAN, SPAN), 1)
    causal = (row_pos >= col_pos).astype(jnp.float32)
    pair_mask = (seq_blocks[:, :, None] == seq_blocks[:, None, :]).astype(jnp.float32) * causal[
        None
    ]
    intersection = jnp.einsum("cqn,csn->cqs", query_out, keys_in, precision=lax.Precision.HIGHEST)
    gaps = running[:, :, :, None] - running[:, :, None, :]
    decays = jnp.exp(gaps * pair_mask[:, None]) * pair_mask[:, None]
    mixing = decays * intersection[:, None]
    inner_out = jnp.einsum("chqs,cshp->cqhp", mixing, scaled, precision=lax.Precision.HIGHEST)
    last_seq = seq_blocks[:, -1]
    end_total = running[:, :, -1]
    tail_mask = (seq_blocks == last_seq[:, None]).astype(jnp.float32)
    to_end = jnp.exp((end_total[:, :, None] - running) * tail_mask[:, None]) * tail_mask[:, None]
    block_state = jnp.einsum(
        "csn,chs,cshp->chnp", keys_in, to_end, scaled, precision=lax.Precision.HIGHEST
    )
    prior_seq = jnp.concatenate([jnp.full((1,), -2, jnp.int32), last_seq[:-1]])
    carried = (last_seq == prior_seq).astype(jnp.float32)

    def advance(state, inputs):
        fresh, factor, flag = inputs
        return (state * factor[:, None, None] * flag + fresh, state)

    _, incoming = lax.scan(
        advance, jnp.zeros((NH, NS, HD), jnp.float32), (block_state, jnp.exp(end_total), carried)
    )
    entering = (seq_blocks == prior_seq[:, None]).astype(jnp.float32)
    from_state = jnp.einsum("cqn,chnp->cqhp", query_out, incoming, precision=lax.Precision.HIGHEST)
    growth = jnp.exp(running).transpose(0, 2, 1) * entering[:, :, None]
    result = (inner_out + from_state * growth[:, :, :, None]).reshape(length, NH, HD)
    result = result + skip_gain[None, :, None] * values.reshape(length, NH, HD)
    gated = result.reshape(length, DI) * jax.nn.silu(gate_part)
    scale = lax.rsqrt(jnp.mean(gated * gated, axis=-1, keepdims=True) + EPS)
    return gated * scale * out_scale[None, :] * live_rows[:, None]


def per_device(
    hidden_in,
    cotangent,
    seq_ids,
    norm_gain,
    in_weight,
    conv_weight,
    conv_bias,
    out_gain,
    out_weight,
    decay_log,
    skip_gain,
    step_bias,
):
    contract_rows = (((0,), (0,)), ((), ()))
    contract_cols = (((1,), (1,)), ((), ()))
    full_norm, full_in, full_kernel, full_shift, full_gate, full_out = (
        lax.all_gather(norm_gain, ("dp", "fsdp"), axis=0, tiled=True),
        lax.all_gather(in_weight, ("dp", "fsdp"), axis=0, tiled=True),
        lax.all_gather(conv_weight, ("dp", "fsdp"), axis=1, tiled=True),
        lax.all_gather(conv_bias, ("dp", "fsdp"), axis=0, tiled=True),
        lax.all_gather(out_gain, ("dp", "fsdp"), axis=0, tiled=True),
        lax.all_gather(out_weight, ("dp", "fsdp"), axis=0, tiled=True),
    )
    normed, norm_pull = jax.vjp(norm_input, hidden_in, full_norm.astype(jnp.float32))
    normed_b = normed.astype(jnp.bfloat16)
    projected = jnp.dot(normed_b, full_in, preferred_element_type=jnp.float32)
    mixed_out, mix_pull = jax.vjp(
        partial(mixer, seq_index=seq_ids),
        projected,
        full_kernel.astype(jnp.float32),
        full_shift.astype(jnp.float32),
        full_gate.astype(jnp.float32),
        decay_log,
        skip_gain,
        step_bias,
    )
    mixed_b = mixed_out.astype(jnp.bfloat16)
    block_out = hidden_in + jnp.dot(mixed_b, full_out, preferred_element_type=jnp.float32)
    back_in, back_out = (
        lax.all_gather(in_weight, ("dp", "fsdp"), axis=0, tiled=True),
        lax.all_gather(out_weight, ("dp", "fsdp"), axis=0, tiled=True),
    )
    upstream_b = cotangent.astype(jnp.bfloat16)
    grad_wout = lax.dot_general(
        mixed_b, upstream_b, contract_rows, preferred_element_type=jnp.float32
    )
    d_mixed = lax.dot_general(
        upstream_b, back_out, contract_cols, preferred_element_type=jnp.float32
    )
    d_proj, grad_kernel, grad_shift, grad_gate, grad_decay, grad_skip, grad_step = mix_pull(d_mixed)
    d_proj_b = d_proj.astype(jnp.bfloat16)
    grad_win = lax.dot_general(
        normed_b, d_proj_b, contract_rows, preferred_element_type=jnp.float32
    )
    d_normed = lax.dot_general(d_proj_b, back_in, contract_cols, preferred_element_type=jnp.float32)
    d_hidden, grad_gain = norm_pull(d_normed)
    grad_hidden = cotangent + d_hidden
    outer = (
        lax.psum_scatter(
            grad_gain.astype(jnp.bfloat16), "dp", scatter_dimension=0, tiled=True
        ).astype(jnp.float32),
        lax.psum_scatter(
            grad_win.astype(jnp.bfloat16), "dp", scatter_dimension=0, tiled=True
        ).astype(jnp.float32),
        lax.psum_scatter(
            grad_kernel.astype(jnp.bfloat16), "dp", scatter_dimension=1, tiled=True
        ).astype(jnp.float32),
        lax.psum_scatter(
            grad_shift.astype(jnp.bfloat16), "dp", scatter_dimension=0, tiled=True
        ).astype(jnp.float32),
        lax.psum_scatter(
            grad_gate.astype(jnp.bfloat16), "dp", scatter_dimension=0, tiled=True
        ).astype(jnp.float32),
        lax.psum_scatter(
            grad_wout.astype(jnp.bfloat16), "dp", scatter_dimension=0, tiled=True
        ).astype(jnp.float32),
    )
    owned = (
        lax.psum_scatter(
            outer[0].astype(jnp.bfloat16), "fsdp", scatter_dimension=0, tiled=True
        ).astype(jnp.float32),
        lax.psum_scatter(
            outer[1].astype(jnp.bfloat16), "fsdp", scatter_dimension=0, tiled=True
        ).astype(jnp.float32),
        lax.psum_scatter(
            outer[2].astype(jnp.bfloat16), "fsdp", scatter_dimension=1, tiled=True
        ).astype(jnp.float32),
        lax.psum_scatter(
            outer[3].astype(jnp.bfloat16), "fsdp", scatter_dimension=0, tiled=True
        ).astype(jnp.float32),
        lax.psum_scatter(
            outer[4].astype(jnp.bfloat16), "fsdp", scatter_dimension=0, tiled=True
        ).astype(jnp.float32),
        lax.psum_scatter(
            outer[5].astype(jnp.bfloat16), "fsdp", scatter_dimension=0, tiled=True
        ).astype(jnp.float32),
    )
    head_sums = lax.psum((grad_decay, grad_skip, grad_step), ("dp", "fsdp"))
    return (
        block_out,
        grad_hidden,
        owned[0],
        owned[1],
        owned[2],
        owned[3],
        owned[4],
        owned[5],
        head_sums[0],
        head_sums[1],
        head_sums[2],
    )


def solution(mesh):
    in_specs = (
        P(("dp", "fsdp"), None),
        P(("dp", "fsdp"), None),
        P(("dp", "fsdp")),
        P(("dp", "fsdp")),
        P(("dp", "fsdp"), None),
        P(None, ("dp", "fsdp")),
        P(("dp", "fsdp")),
        P(("dp", "fsdp")),
        P(("dp", "fsdp"), None),
        P(),
        P(),
        P(),
    )
    out_specs = (
        P(("dp", "fsdp"), None),
        P(("dp", "fsdp"), None),
        P(("dp", "fsdp")),
        P(("dp", "fsdp"), None),
        P(None, ("dp", "fsdp")),
        P(("dp", "fsdp")),
        P(("dp", "fsdp")),
        P(("dp", "fsdp"), None),
        P(),
        P(),
        P(),
    )
    return jax.shard_map(
        per_device, mesh=mesh, in_specs=in_specs, out_specs=out_specs, check_vma=False
    )
```

profile of v0, /device:TPU:0, one launch (start us, length us, event | category | flops | bytes accessed | tf_op | source)
XLA Modules:
  0.0 543.5 jit_solution(14664170534759224089)
XLA Ops:
  8.7 1.3 slice.93
  17.3 1.3 multiply_reduce_fusion.13
  20.6 1.3 compare_convert_fusion.1
  24.4 42.9 %all-reduce.31 = (bf16[768]{0:T(1024)(128)(2,1)S(1)}, bf16[1792]{0:T(1024)(128)(2,1)S(1)}, bf16[1536]{0:T(1024)(128)(2,1)S(1)}) all-reduce(bf16[768]{0:T(1024)(128)(2,1)S(1)} %dynamic-update-slice.1, bf16[1792]{0:T(1024)(128)(2,1)S(1)} %dynamic-update-slice, ...), channel_id=1, replica_groups=mesh['dp'=8,'fsdp'=4] {'dp','fsdp'}, use_global_device_ids=true, to_apply=%add.20 | all-reduce | flops 4096 | bytes 16384
  68.7 40.9 %all-gather = bf16[32,56,4]{1,2,0:T(4,128)(2,1)S(1)} all-gather(bf16[1,56,4]{1,2,0:T(4,128)(2,1)} %bitcast.207), channel_id=1, replica_groups=mesh['dp'=8,'fsdp'=4] {'dp','fsdp'}, dimensions={0}, use_global_device_ids=true | all-gather | bytes 14784 | tf_op jit(solution)/shard_map/all_gather | solution.py:110
  109.9 1.5 compare_select_fusion
  111.4 5.1 fusion.86
  116.5 1.5 slice.102
  118.0 1.4 slice.100
  119.4 1.4 slice.98
  121.5 6.4 %fusion.20 = (f32[256,1792]{0,1:T(8,128)S(1)}, f32[256,1792]{0,1:T(8,128)}) fusion(f32[1792]{0:T(1024)S(1)} %get-tuple-element.383, f32[256]{0:T(256)S(1)} %get-tuple-element.453, f32[253,1792]{0,1:T(8,128)} %slice.102, f32[1792]{0:T(1024)S(1)} %get-tuple-element.384, f32[256]{0:T(256)S(1)} %pad_convert_fusion.1, f32[254,1792]{0,1:T(8,128)} %slice.100, ...), kind=kLoop, calls=%fused_computation.48 | loop fusion | flops 6881280 | bytes 11005952 | tf_op jit(solution)/shard_map/jvp(jit(silu))/mul | solution.py:41
  133.8 2.9 reshape.237
  136.7 4.1 convolution_bitcast_fusion.1
  140.8 2.0 broadcast.176.clone
  142.9 23.0 %while.34 = (s32[]{:T(128)}, f32[24,128,64]{2,1,0:T(8,128)S(1)}, f32[2,24,128,64]{3,2,1,0:T(8,128)}, f32[2,24,1,1]{1,3,2,0:T(1,128)}, f32[2,24]{1,0:T(2,128)}, /...) while((s32[]{:T(128)}, f32[24,128,64]{2,1,0:T(8,128)S(1)}, ...), condition=%wide.region_3.4_spmd.clone, body=%wide.region_2.3_spmd.clone.sunk | while | flops 983043 | bytes 11011944 | solution.py:78
  146.5 2.1 constant_dynamic-slice_fusion.6
  148.5 2.7 copy.351
  151.3 1.3 bitcast_dynamic-update-slice_fusion.4
  157.9 2.1 constant_dynamic-slice_fusion.6
  160.0 2.7 copy.351
  165.8 2.6 copy.244
  169.2 1.3 fusion.95
  170.5 1.4 fusion.96
  173.1 6.4 %bitcast_add_fusion.4 = f32[2,128,24,64]{1,3,2,0:T(8,128)S(1)} fusion(f32[2,128,24,64]{1,3,2,0:T(8,128)S(1)} %bitcast.186, f32[2,128,128]{2,1,0:T(8,128)S(1)} %fusion.95, f32[2,128,128]{2,1,0:T(8,128)S(1)} %copy-done.45, f32[2,24,128]{2,1,0:T(8,128)S(1)} %bitcast.194, f32[2,128,24,64]{1,0,3,2:T(2,128)S(1)} %copy-done.12, ...), kind=kOutput, calls=%fused_computation.64 | convolution fusion | flops 608305152 | bytes 5054464 | tf_op jit(solution)/shard_map/jvp(chqs,cshp->cqhp)/dot_general | solution.py:63
  181.0 2.4 multiply_reduce_fusion.10
  184.5 2.3 convolution_convert_fusion.1
  186.8 3.6 multiply_reduce_fusion.7
  190.5 4.7 multiply_reduce_fusion.6
  195.2 2.5 reshape.243
  197.8 8.4 %fusion.52 = f32[2,128,128]{2,1,0:T(8,128)} fusion(f32[2,24,128,64]{3,2,1,0:T(8,128)} %get-tuple-element.584, f32[2,128,24,64]{1,0,3,2:T(2,128)S(1)} %reshape.243, f32[2,128,24]{1,2,0:T(8,128)} %copy-done.41), kind=kOutput, calls=%fused_computation.96 | convolution fusion | flops 604372992 | bytes 3301376 | tf_op jit(solution)/shard_map/transpose(jvp(cqn,chnp->cqhp))/dot_general | solution.py:82
  206.2 7.9 %fusion.14 = (f32[2,24,128]{2,1,0:T(8,128)}, f32[2,24,128]{2,1,0:T(8,128)}, f32[2,128,128]{2,1,0:T(8,128)}) fusion(f32[2,128,128]{2,1,0:T(8,128)S(1)} %copy-done.44, f32[2,128,128]{2,1,0:T(8,128)S(1)} %copy-done.46, f32[2,24,128]{2,1,0:T(8,128)S(1)} %bitcast.195, f32[2,128,24,64]{1,0,3,2:T(2,128)S(1)} %copy-done.13, f32[2,128,24]{1,2,0:T(8,128)S(1)} %copy-done.36, ...), kind=kOutput, calls=%fused_computation.33 | convolution fusion | flops 612978688 | bytes 3637248 | tf_op jit(solution)/shard_map/transpose(jvp(chqs,cshp->cqhp))/dot_general | solution.py:63
  214.1 2.6 convolution_bitcast_fusion
  216.7 2.1 broadcast.176
  218.8 16.1 %while.35 = (s32[]{:T(128)}, f32[24,128,64]{2,1,0:T(8,128)S(1)}, f32[2,24,128,64]{3,2,1,0:T(8,128)}, f32[2,24]{1,0:T(2,128)S(1)}, f32[2,24,128,64]{2,3,1,0:T(8,1...) while((s32[]{:T(128)}, f32[24,128,64]{2,1,0:T(8,128)S(1)}, ...), condition=%wide.region_8.9_spmd.clone, body=%wide.region_6.8_spmd.clone.sunk | while | flops 1376236 | bytes 14942980 | solution.py:78
  219.4 2.1 constant_dynamic-slice_fusion.7
  221.5 1.6 copy.352
  223.1 1.3 bitcast_dynamic-update-slice_fusion.5
  227.4 2.1 constant_dynamic-slice_fusion.7
  229.5 1.6 copy.352
  231.1 1.3 bitcast_dynamic-update-slice_fusion.5
  235.0 8.4 %fusion.55 = f32[2,128,128]{2,1,0:T(8,128)} fusion(f32[2,24,128,64]{3,2,1,0:T(8,128)} %get-tuple-element.212, f32[2,128,24,64]{1,0,3,2:T(2,128)} %reshape.237, f32[2,128,24]{1,2,0:T(8,128)S(1)} %copy-done.40, f32[2,128,24]{1,2,0:T(8,128)S(1)} %copy-done.37), kind=kOutput, calls=%fused_computation.97 | convolution fusion | flops 604766208 | bytes 3325952 | tf_op jit(solution)/shard_map/transpose(jvp(csn,chs,cshp->chnp))/dot_general | solution.py:68
  243.4 5.1 multiply_reduce_fusion.5
  249.4 1.9 convolution_add_fusion.2
  251.3 1.7 copy.291
  253.0 4.5 bitcast_add_fusion.3
  259.6 1.4 fusion.23
  262.0 1.7 copy.292
  265.6 3.9 reduce_window_sum.23
  270.5 2.2 fusion.24
  272.7 1.4 fusion.89
  274.1 6.4 %fusion.88 = (bf16[1792]{0:T(1024)(128)(2,1)S(1)}, f32[1792]{0:T(1024)S(1)}, f32[1792]{0:T(1024)S(1)}, f32[1792]{0:T(1024)S(1)}, f32[1792]{0:T(1024)S(1)}, /*index=5*/f32[256,1792]{0,1:T(8,128)S(1)}) fusion(f32[256,3352]{0,1:T(8,128)S(1)} %copy-done.3, f32[256]{0:T(256)S(1)} %copy-done.72, f32[255,1792]{0,1:T(8,128)} %slice.98, f32[256]{0:T(256)S(1)} %copy-done.82, ...), kind=kLoop, calls=%fused_computation.176 | loop fusion | flops 10542336 | bytes 12837376 | tf_op jit(solution)/shard_map/transpose(jvp())/reduce_sum | solution.py:33
  285.3 4.1 convolution_convert_fusion
  296.6 37.6 %all-reduce.30 = (f32[24]{0:T(128)}, f32[24]{0:T(128)}, f32[24]{0:T(128)}) all-reduce(f32[24]{0:T(128)S(1)} %negate_multiply_fusion, f32[24]{0:T(128)S(1)} %reduce_sum.242, f32[24]{0:T(128)S(1)} %get-tuple-element.429), channel_id=1, replica_groups=mesh['dp'=8,'fsdp'=4] {'dp','fsdp'}, use_global_device_ids=true, to_apply=%region_37.38 | all-reduce | flops 72 | bytes 576 | tf_op jit(solution)/shard_map/psum | solution.py:189
  334.4 6.3 %multiply_reduce_fusion.11 = (bf16[768]{0:T(1024)(128)(2,1)S(1)}, f32[256]{0:T(256)S(1)}, f32[256,768]{1,0:T(8,128)}) fusion(f32[256,768]{1,0:T(8,128)S(1)} %copy-done.15, f32[256]{0:T(256)S(1)} %copy-done.65, f32[768]{0:T(1024)S(1)} %convert_element_type.104, bf16[768,3352]{1,0:T(8,128)(2,1)} %all-gather.4.cloned.1.call-done, ...), kind=kOutput, calls=%fused_computation.101 | convolution fusion | flops 1321812992 | bytes 10160640 | tf_op jit(solution)/shard_map/dot_general | solution.py:146
  340.7 38.4 %all-reduce.32 = (bf16[768]{0:T(1024)(128)(2,1)S(1)}, bf16[1792]{0:T(1024)(128)(2,1)S(1)}, bf16[1536]{0:T(1024)(128)(2,1)S(1)}) all-reduce(bf16[768]{0:T(1024)(128)(2,1)S(1)} %get-tuple-element.380, bf16[1792]{0:T(1024)(128)(2,1)S(1)} %get-tuple-element.375, ...), channel_id=2, replica_groups=mesh['dp'=8,'fsdp'=4] {'dp'}, use_global_device_ids=true, to_apply=%region_18.19.clone | all-reduce | flops 4096 | bytes 16384
  379.3 43.4 %reduce-scatter.11.cloned.1.call-done = bf16[96,3352]{1,0:T(8,128)(2,1)} async-done(((bf16[768,3352]{1,0:T(8,128)(2,1)}), bf16[96,3352]{1,0:T(8,128)(2,1)}) %reduce-scatter.11.cloned.1.call-update) | async-done | bytes 643600 | tf_op jit(solution)/shard_map/reduce_scatter | solution.py:153
  422.7 2.6 fusion.60
  425.3 1.9 convolution_add_fusion
  427.2 60.7 %reduce-scatter.17.cloned.1.call-done = bf16[224,4]{1,0:T(8,128)(2,1)} async-done(((bf16[1792,4]{1,0:T(8,128)(2,1)}), bf16[224,4]{1,0:T(8,128)(2,1)}) %reduce-scatter.17.cloned.1.call-update) | async-done | bytes 1808
  488.8 5.7 %all-reduce.33 = (bf16[96]{0:T(256)(128)(2,1)S(1)}, bf16[4,224]{1,0:T(4,128)(2,1)S(1)}, bf16[224]{0:T(256)(128)(2,1)S(1)}, bf16[192]{0:T(256)(128)(2,1)S(1)}) all-reduce(bf16[96]{0:T(256)(128)(2,1)S(1)} %dynamic-slice.1, bf16[4,224]{1,0:T(4,128)(2,1)S(1)} %copy.294, ...), channel_id=3, replica_groups=mesh['dp'=8,'fsdp'=4] {'fsdp'}, use_global_device_ids=true, to_apply=%region_19.20.clone | all-reduce | flops 1408 | bytes 5632
  496.9 12.7 %reduce-scatter.15.cloned.1.call-done = bf16[48,768]{1,0:T(8,128)(2,1)} async-done(((bf16[192,768]{1,0:T(8,128)(2,1)}), bf16[48,768]{1,0:T(8,128)(2,1)}) %reduce-scatter.15.cloned.1.call-update) | async-done | bytes 73744 | tf_op jit(solution)/shard_map/reduce_scatter | solution.py:185
  509.6 1.6 convert_element_type.127
  511.2 23.3 %reduce-scatter.19.cloned.1.call-done = bf16[24,3352]{1,0:T(8,128)(2,1)} async-done(((bf16[96,3352]{1,0:T(8,128)(2,1)}), bf16[24,3352]{1,0:T(8,128)(2,1)}) %reduce-scatter.19.cloned.1.call-update) | async-done | bytes 160912
  534.5 1.7 convert_element_type.119
  (313 shorter events, 62.1 us)
Async XLA Ops:
  7.2 104.2 %all-gather.4.cloned.1.call-start = ((), (), s32[]{:S(2)}) async-start(), calls=%async_computation.5 | async-start | bytes 5474304 | tf_op jit(solution)/shard_map/all_gather | solution.py:109
  7.9 178.9 %all-gather.6.cloned.1.call-start = ((), (), s32[]{:S(2)}) async-start(), calls=%async_computation.6 | async-start | bytes 2433024 | tf_op jit(solution)/shard_map/all_gather | solution.py:113
  8.7 325.6 %reduce-scatter.13.cloned.1.call-start = ((), (), s32[]{:S(2)}) async-start(), calls=%async_computation.8 | async-start | bytes 2654208 | tf_op jit(solution)/shard_map/reduce_scatter | solution.py:165
  15.2 105.6 %copy-start.87 = (f32[24]{0:T(128)}, f32[24]{0:T(128)S(1)}, u32[]{:S(2)}) copy-start(f32[24]{0:T(128)S(1)} %exponential_negate_fusion) | copy-start | bytes 292
  17.3 104.2 %copy-start.81 = (f32[256]{0:T(256)}, f32[256]{0:T(256)S(1)}, u32[]{:S(2)}) copy-start(f32[256]{0:T(256)S(1)} %pad_convert_fusion.1) | copy-start | bytes 3076
  18.5 4.2 copy-start.76
  18.6 97.9 %copy-start.64 = (f32[256]{0:T(256)}, f32[256]{0:T(256)S(1)}, u32[]{:S(2)}) copy-start(f32[256]{0:T(256)S(1)} %fusion.84) | copy-start | bytes 3076
  19.3 102.2 %copy-start.71 = (f32[256]{0:T(256)}, f32[256]{0:T(256)S(1)}, u32[]{:S(2)}) copy-start(f32[256]{0:T(256)S(1)} %get-tuple-element.452) | copy-start | bytes 3076
  19.3 102.2 %copy-start.73 = (f32[256]{0:T(256)}, f32[256]{0:T(256)S(1)}, u32[]{:S(2)}) copy-start(f32[256]{0:T(256)S(1)} %get-tuple-element.453) | copy-start | bytes 3076
  21.9 106.8 %copy-start.68 = (f32[2,128]{1,0:T(2,128)}, f32[2,128]{1,0:T(2,128)S(1)}, u32[]{:S(2)}) copy-start(f32[2,128]{1,0:T(2,128)S(1)} %get-tuple-element.447) | copy-start | bytes 3076
  109.9 11.6 %copy-start.50 = (f32[1792]{0:T(1024)}, f32[1792]{0:T(1024)S(1)}, u32[]{:S(2)}) copy-start(f32[1792]{0:T(1024)S(1)} %get-tuple-element.383) | copy-start | bytes 21508
  109.9 11.6 %copy-start.52 = (f32[1792]{0:T(1024)}, f32[1792]{0:T(1024)S(1)}, u32[]{:S(2)}) copy-start(f32[1792]{0:T(1024)S(1)} %get-tuple-element.384) | copy-start | bytes 21508
  109.9 11.6 %copy-start.54 = (f32[1792]{0:T(1024)}, f32[1792]{0:T(1024)S(1)}, u32[]{:S(2)}) copy-start(f32[1792]{0:T(1024)S(1)} %get-tuple-element.385) | copy-start | bytes 21508
  109.9 11.6 %copy-start.56 = (f32[1792]{0:T(1024)}, f32[1792]{0:T(1024)S(1)}, u32[]{:S(2)}) copy-start(f32[1792]{0:T(1024)S(1)} %get-tuple-element.382) | copy-start | bytes 21508
  116.5 4.3 copy-start.2
  120.9 8.4 %copy-start.38 = (f32[256,24]{0,1:T(8,128)}, f32[256,24]{0,1:T(8,128)S(1)}, u32[]{:S(2)}) copy-start(f32[256,24]{0,1:T(8,128)S(1)} %get-tuple-element.437) | copy-start | bytes 73732
  121.3 7.3 %copy-start.27 = (f32[2,128,24]{1,2,0:T(8,128)}, f32[2,128,24]{1,2,0:T(8,128)S(1)}, u32[]{:S(2)}) copy-start(f32[2,128,24]{1,2,0:T(8,128)S(1)} %copy.238) | copy-start | bytes 73732
  127.9 3.9 copy-start.7
  169.1 2.8 copy-start.41
  170.5 2.6 copy-start.12
  170.5 2.6 copy-start.28
  180.7 2.6 copy-start.17
  181.0 3.6 copy-start.21
  181.0 3.6 copy-start.62
  183.4 7.1 %copy-start.4 = (f32[256,1536]{0,1:T(8,128)}, f32[256,1536]{0,1:T(8,128)S(1)}, u32[]{:S(2)}) copy-start(f32[256,1536]{0,1:T(8,128)S(1)} %get-tuple-element.435) | copy-start | bytes 4718596
  186.8 3.6 copy-start.80
  186.8 3.7 copy-start.9
  186.8 3.7 copy-start.18
  186.8 3.7 copy-start.48
  186.8 3.7 copy-start.59
  197.7 16.4 %copy-start.10 = (f32[2,128,24,64]{1,0,3,2:T(2,128)}, f32[2,128,24,64]{1,0,3,2:T(2,128)S(1)}, u32[]{:S(2)}) copy-start(f32[2,128,24,64]{1,0,3,2:T(2,128)S(1)} %reshape.243) | copy-start | bytes 4718596
  197.7 8.4 %copy-start.13 = (f32[2,128,24,64]{1,0,3,2:T(2,128)S(1)}, f32[2,128,24,64]{1,0,3,2:T(2,128)}, u32[]{:S(2)}) copy-start(f32[2,128,24,64]{1,0,3,2:T(2,128)} %reshape.237) | copy-start | bytes 4718596
  197.7 8.4 %copy-start.29 = (f32[2,128,24]{1,2,0:T(8,128)S(1)}, f32[2,128,24]{1,2,0:T(8,128)}, u32[]{:S(2)}) copy-start(f32[2,128,24]{1,2,0:T(8,128)} %copy-done.27) | copy-start | bytes 73732
  197.7 8.4 %copy-start.36 = (f32[2,128,24]{1,2,0:T(8,128)S(1)}, f32[2,128,24]{1,2,0:T(8,128)}, u32[]{:S(2)}) copy-start(f32[2,128,24]{1,2,0:T(8,128)} %copy_bitcast_fusion) | copy-start | bytes 73732
  197.7 8.4 %copy-start.44 = (f32[2,128,128]{2,1,0:T(8,128)S(1)}, f32[2,128,128]{2,1,0:T(8,128)}, u32[]{:S(2)}) copy-start(f32[2,128,128]{2,1,0:T(8,128)} %copy-done.43) | copy-start | bytes 393220
  197.7 8.4 %copy-start.46 = (f32[2,128,128]{2,1,0:T(8,128)S(1)}, f32[2,128,128]{2,1,0:T(8,128)}, u32[]{:S(2)}) copy-start(f32[2,128,128]{2,1,0:T(8,128)} %compare_select_fusion) | copy-start | bytes 393220
  206.2 7.9 %copy-start.42 = (f32[2,128,24]{1,2,0:T(8,128)S(1)}, f32[2,128,24]{1,2,0:T(8,128)}, u32[]{:S(2)}) copy-start(f32[2,128,24]{1,2,0:T(8,128)} %copy-done.41) | copy-start | bytes 73732
  218.8 16.1 %copy-start.37 = (f32[2,128,24]{1,2,0:T(8,128)S(1)}, f32[2,128,24]{1,2,0:T(8,128)}, u32[]{:S(2)}) copy-start(f32[2,128,24]{1,2,0:T(8,128)} %copy_bitcast_fusion) | copy-start | bytes 73732
  218.8 16.1 %copy-start.40 = (f32[2,128,24]{1,2,0:T(8,128)S(1)}, f32[2,128,24]{1,2,0:T(8,128)}, u32[]{:S(2)}) copy-start(f32[2,128,24]{1,2,0:T(8,128)} %multiply_bitcast_fusion) | copy-start | bytes 73732
  235.0 8.4 %copy-start.6 = (f32[2,24,128,64]{3,2,1,0:T(8,128)S(1)}, f32[2,24,128,64]{3,2,1,0:T(8,128)}, u32[]{:S(2)}) copy-start(f32[2,24,128,64]{3,2,1,0:T(8,128)} %get-tuple-element.212) | copy-start | bytes 4718596
  235.0 8.4 %copy-start.14 = (f32[2,128,24,64]{1,0,3,2:T(2,128)S(1)}, f32[2,128,24,64]{1,0,3,2:T(2,128)}, u32[]{:S(2)}) copy-start(f32[2,128,24,64]{1,0,3,2:T(2,128)} %reshape.237) | copy-start | bytes 4718596
  248.5 4.5 copy-start.11
  248.5 4.5 copy-start.30
  248.6 174.1 %reduce-scatter.11.cloned.1.call-start = ((), (), s32[]{:S(2)}) async-start(), calls=%async_computation.7 | async-start | bytes 5971968 | tf_op jit(solution)/shard_map/reduce_scatter | solution.py:153
  259.5 4.2 copy-start.69
  259.5 4.4 copy-start.23
  265.6 7.1 %copy-start.3 = (f32[256,3352]{0,1:T(8,128)S(1)}, f32[256,3352]{0,1:T(8,128)}, u32[]{:S(2)}) copy-start(f32[256,3352]{0,1:T(8,128)} %copy-done.2) | copy-start | bytes 10297348
  270.5 3.6 copy-start.31
  270.5 3.6 copy-start.32
  270.5 3.6 copy-start.72
  270.5 3.6 copy-start.74
  270.5 3.6 copy-start.82
  274.1 6.4 %copy-start.55 = (f32[1792]{0:T(1024)S(1)}, f32[1792]{0:T(1024)}, u32[]{:S(2)}) copy-start(f32[1792]{0:T(1024)} %copy-done.54) | copy-start | bytes 21508
  274.1 6.4 %copy-start.85 = (f32[255]{0:T(256)S(1)}, f32[255]{0:T(256)}, u32[]{:S(2)}) copy-start(f32[255]{0:T(256)} %slice.112) | copy-start | bytes 3064
  289.5 3.2 copy-start.92
  289.5 6.9 %copy-start.88 = (f32[24]{0:T(128)S(1)}, f32[24]{0:T(128)}, u32[]{:S(2)}) copy-start(f32[24]{0:T(128)} %get-tuple-element.445) | copy-start | bytes 292
  289.5 6.9 %copy-start.90 = (f32[24]{0:T(128)S(1)}, f32[24]{0:T(128)}, u32[]{:S(2)}) copy-start(f32[24]{0:T(128)} %param.25) | copy-start | bytes 292
  289.5 7.0 %copy-start.61 = (f32[1536]{0:T(1024)S(1)}, f32[1536]{0:T(1024)}, u32[]{:S(2)}) copy-start(f32[1536]{0:T(1024)} %get-tuple-element.431) | copy-start | bytes 18436
  289.5 198.4 %reduce-scatter.17.cloned.1.call-start = ((), (), s32[]{:S(2)}) async-start(), calls=%async_computation.10 | async-start | bytes 516096
  296.3 213.3 %reduce-scatter.15.cloned.1.call-start = ((), (), s32[]{:S(2)}) async-start(), calls=%async_computation.9 | async-start | bytes 368640 | tf_op jit(solution)/shard_map/reduce_scatter | solution.py:185
  334.3 6.4 %copy-start.70 = (bf16[1536]{0:T(1024)(128)(2,1)S(1)}, bf16[1536]{0:T(1024)(128)(2,1)}, u32[]{:S(2)}) copy-start(bf16[1536]{0:T(1024)(128)(2,1)} %get-tuple-element.373) | copy-start | bytes 9220
  334.3 88.4 %copy-start.77 = (f32[256]{0:T(256)S(1)}, f32[256]{0:T(256)}, u32[]{:S(2)}) copy-start(f32[256]{0:T(256)} %copy-done.76) | copy-start | bytes 3076
  334.3 200.2 %reduce-scatter.19.cloned.1.call-start = ((), (), s32[]{:S(2)}) async-start(), calls=%async_computation.11 | async-start | bytes 829440
  334.4 90.9 %copy-start.19 = (bf16[1536,768]{1,0:T(8,128)(2,1)S(1)}, bf16[1536,768]{1,0:T(8,128)(2,1)}, u32[]{:S(2)}) copy-start(bf16[1536,768]{1,0:T(8,128)(2,1)} %all-gather.6.cloned.1.call-done) | copy-start | bytes 7077892
  (40 other events, 63.8 us)
Sparse Core Ops, SparseCore 0:
  10.9 68.8 all-gather.3
  82.7 55.8 all-gather.5
  248.7 65.9 reduce-scatter.12
  318.1 104.5 reduce-scatter.10
  425.8 62.1 reduce-scatter.16
  490.3 19.3 reduce-scatter.14
  512.2 22.2 reduce-scatter.18
where the time goes:
time: 553 us; the launch traced here: 543 us
  blocking collectives  165 us (30%)
  waiting for transfers between devices  142 us (26%)
  local copies, waits for them, and re-layouts  77.4 us (14%)
  matrix products  76.4 us (14%)
  other arithmetic  62.2 us (11%)
  between operations  19.6 us (4%)
    unnamed x3, blocking collectives  86.9 us
    unnamed x9, waiting for transfers between devices  85.5 us
    reduce_scatter x1, waiting for transfers between devices, per_device(): lax.psum_scatter(grad_win.astype(jnp.bfloat16), 'dp', scatter_dimension=0...  43.4 us
    all_gather x1, blocking collectives, per_device(): lax.all_gather(conv_weight, ('dp', 'fsdp'), axis=1, tiled=True)  40.9 us
    psum x1, blocking collectives, per_device(): head_sums = lax.psum((grad_decay, grad_skip, grad_step), ('dp', 'fsdp'))  37.6 us
    dynamic_slice x12, local copies, waits for them, and re-layouts, mixer(): lax.scan(advance, jnp.zeros((NH, NS, HD), jnp.float32), (block_state, jnp...  20.7 us
    dot_general x3, matrix products, mixer(): jnp.einsum('chqs,cshp->cqhp', mixing, scaled, precision=lax.Precision.HIG...  18.8 us
    dot_general x3, matrix products, mixer(): jnp.einsum('csn,chs,cshp->chnp', keys_in, to_end, scaled, precision=lax.P...  17.6 us
  transfers between devices with their start and end apart: 7, of which 4 were waited for; matrix products, arithmetic and copies ran while one was open for 27% of the time, Pallas kernels for 0%

commit v1 on v0

v1 whole, which is shorter than its diff:
```python
import jax
import jax.numpy as jnp
from jax import lax
from jax.experimental import pallas as pl
from jax.experimental.pallas import tpu as pltpu
from jax.sharding import PartitionSpec as P

NS = 128
HD = 64
NH = 24
KC = 4
DI = 1536
CONV = 1792
LANE = 128
EPS = 1e-05
AXES = ("dp", "fsdp")
F32 = jnp.float32
BF16 = jnp.bfloat16
HIGH = lax.Precision.HIGHEST
VM = pl.BlockSpec(memory_space=pltpu.VMEM)


def sds(*shape, dtype=F32):
    return jax.ShapeDtypeStruct(shape, dtype)


def cols(k, width=LANE):
    return pl.ds(pl.multiple_of(k * width, LANE), width)


def sigmoid(x):
    return 1.0 / (1.0 + jnp.exp(-x))


def dot(a, b, dims=((1,), (0,)), precision=None):
    return lax.dot_general(
        a, b, (dims, ((), ())), precision=precision, preferred_element_type=F32
    )


def pair_masks():
    lane = lax.broadcasted_iota(jnp.int32, (1, LANE), 1)
    first = (lane < HD).astype(F32)
    return first, 1.0 - first


def spread(width_from, k):
    head = lax.broadcasted_iota(jnp.int32, (width_from, LANE), 0)
    lane = lax.broadcasted_iota(jnp.int32, (width_from, LANE), 1)
    return (head == 2 * k + lane // HD).astype(F32)


def pair_decay(cum_e, cum_t, k, mask):
    two = cum_e[:, cols(k)]
    low = jnp.float32(-1e30)
    first = two[:, 0:1] - cum_t[pl.ds(2 * k, 1), :]
    second = two[:, HD : HD + 1] - cum_t[pl.ds(2 * k + 1, 1), :]
    return jnp.exp(jnp.where(mask, first, low)), jnp.exp(jnp.where(mask, second, low))


def same_mask(seq_col, seq_row):
    n = seq_col.shape[0]
    row = lax.broadcasted_iota(jnp.int32, (n, n), 0)
    col = lax.broadcasted_iota(jnp.int32, (n, n), 1)
    return (seq_col[...] == seq_row[...]) & (row >= col)


def forward_kernel(
    hidden, w_in, gain, taps, out_gain, skip_e, heads, meta, seq_col, seq_row,
    normed_b, proj, act, d_act, inner, mixed_b, gated, stats, step, step_e, cum_e, cum_t, scores,
):
    h = hidden[...]
    n, d = h.shape
    root = lax.rsqrt(jnp.sum(h * h, axis=-1, keepdims=True) / d + EPS)
    nb = (h * root * gain[...]).astype(BF16)
    normed_b[...] = nb
    wide = 3 * LANE

    @pl.loop(0, proj.shape[1] // wide)
    def _(k):
        proj[:, cols(k, wide)] = dot(nb, w_in[:, cols(k, wide)])

    same = [meta[:, j : j + 1] for j in range(KC - 1)]

    @pl.loop(0, CONV // LANE)
    def _(k):
        x = proj[:, cols(k + DI // LANE)]
        tap = taps[:, cols(k)]
        total = tap[KC : KC + 1] + x * tap[KC - 1 : KC]
        for j in range(1, KC):
            total = total + pltpu.roll(x, j, 0) * same[j - 1] * tap[KC - 1 - j : KC - j]
        sg = sigmoid(total)
        act[:, cols(k)] = total * sg
        d_act[:, cols(k)] = sg * (1.0 + total * (1.0 - sg))

    mask = same_mask(seq_col, seq_row)
    raw = proj[:, DI + CONV : DI + CONV + LANE] + heads[0:1]
    lane = lax.broadcasted_iota(jnp.int32, (1, LANE), 1)
    size = jnp.where(
        lane < NH, jnp.maximum(raw, 0.0) + jnp.log1p(jnp.exp(-jnp.abs(raw))), 0.0
    )
    step[...] = size
    running = dot(mask.astype(F32), size * heads[1:2], precision=HIGH)
    cum_t[...] = running.T
    b = act[:, DI : DI + NS].astype(BF16)
    c = act[:, DI + NS : DI + 2 * NS].astype(BF16)
    scores[...] = dot(c, b, ((1,), (1,)))
    first, second = pair_masks()
    stats[...] = jnp.zeros_like(stats)

    @pl.loop(0, NH // 2)
    def _(k):
        e = spread(LANE, k)
        cum_e[:, cols(k)] = dot(running, e, precision=HIGH)
        size_e = dot(size, e, precision=HIGH)
        step_e[:, cols(k)] = size_e
        decay0, decay1 = pair_decay(cum_e, cum_t, k, mask)
        v = act[:, cols(k)]
        x = v * size_e
        s = scores[...]
        y = dot((s * decay0).astype(BF16), (x * first).astype(BF16)) + dot(
            (s * decay1).astype(BF16), (x * second).astype(BF16)
        )
        inner[:, cols(k)] = y
        g = proj[:, cols(k)]
        z = (y + skip_e[:, cols(k)] * v) * g * sigmoid(g)
        gated[:, cols(k)] = z
        stats[...] += z * z

    scale = lax.rsqrt(jnp.sum(stats[...], axis=-1, keepdims=True) / DI + EPS)
    live = meta[:, KC - 1 : KC]
    stats[...] = jnp.where(lane < HD, scale, root)
    factor = scale * live

    @pl.loop(0, NH // 2)
    def _(k):
        mixed_b[:, cols(k)] = (gated[:, cols(k)] * factor * out_gain[:, cols(k)]).astype(BF16)


def backward_kernel(
    hidden, upstream, w_in, w_out, gain, taps, out_gain, skip_e, heads, meta, seq_col, seq_row,
    proj, act, d_act, inner, gated, stats, step, step_e, cum_e, cum_t, scores,
    grad_hidden, d_proj_b, g_gain, g_taps, g_out, g_heads,
    d_val, d_gated, acc, d_scores,
):
    h = hidden[...]
    n, d = h.shape
    up = upstream[...].astype(BF16)
    mask = same_mask(seq_col, seq_row)
    live = meta[:, KC - 1 : KC]
    scale = stats[:, 0:1]
    root = stats[:, HD : HD + 1]
    first, second = pair_masks()
    acc[...] = jnp.zeros_like(acc)

    @pl.loop(0, NH // 2)
    def _(k):
        dm = dot(up, w_out[cols(k), :], ((1,), (1,))) * live
        z = gated[:, cols(k)]
        g_out[:, cols(k)] = jnp.sum(dm * z * scale, axis=0, keepdims=True)
        u = dm * out_gain[:, cols(k)]
        d_gated[:, cols(k)] = u
        acc[...] += u * z

    pull = jnp.sum(acc[...], axis=-1, keepdims=True) * (scale * scale * scale) / DI
    d_scores[...] = jnp.zeros_like(d_scores)
    g_heads[...] = jnp.zeros_like(g_heads)
    tall = lax.broadcasted_iota(jnp.int32, (8, 1), 0)

    def body(k, carry):
        d_cum, d_step = carry
        e = spread(LANE, k)
        dz = scale * d_gated[:, cols(k)] - gated[:, cols(k)] * pull
        g = proj[:, cols(k)]
        sg = sigmoid(g)
        v = act[:, cols(k)]
        y = inner[:, cols(k)]
        skip = skip_e[:, cols(k)]
        d_proj_b[:, cols(k)] = (
            dz * (y + skip * v) * sg * (1.0 + g * (1.0 - sg))
        ).astype(BF16)
        dy = dz * g * sg
        size_e = step_e[:, cols(k)]
        x = (v * size_e).astype(BF16)
        dyb = dy.astype(BF16)
        dy0 = (dy * first).astype(BF16)
        dy1 = (dy * second).astype(BF16)
        decay0, decay1 = pair_decay(cum_e, cum_t, k, mask)
        s = scores[...]
        dx = dot((s * decay0).astype(BF16), dy0, ((0,), (0,))) + dot(
            (s * decay1).astype(BF16), dy1, ((0,), (0,))
        )
        d_scores[...] += dot(dy0, x, ((1,), (1,))) * decay0 + dot(dy1, x, ((1,), (1,))) * decay1
        d_val[:, cols(k)] = dx * size_e + skip * dy
        flow = dyb.astype(F32) * y - x.astype(F32) * dx
        d_cum = d_cum + dot(flow, e, ((1,), (1,)), precision=HIGH)
        d_step = d_step + dot(dx * v, e, ((1,), (1,)), precision=HIGH)
        skips = jnp.sum(dy * v, axis=0, keepdims=True)
        g_heads[...] += jnp.where(
            tall == 1, dot(jnp.broadcast_to(skips, (8, LANE)), e, ((1,), (1,)), precision=HIGH), 0.0
        )
        return d_cum, d_step

    zero = jnp.zeros((n, LANE), F32)
    d_cum, d_step = lax.fori_loop(0, NH // 2, body, (zero, zero))
    d_rate = dot(mask.astype(F32), d_cum, ((0,), (0,)), precision=HIGH)
    neg = heads[1:2]
    size = step[...]
    raw = proj[:, DI + CONV : DI + CONV + LANE] + heads[0:1]
    lane = lax.broadcasted_iota(jnp.int32, (1, LANE), 1)
    d_raw = jnp.where(lane < NH, (d_step + d_rate * neg) * sigmoid(raw), 0.0)
    d_proj_b[:, DI + CONV : DI + CONV + LANE] = d_raw.astype(BF16)
    g_decay = jnp.sum(d_rate * size * neg, axis=0, keepdims=True)
    g_step = jnp.sum(d_raw, axis=0, keepdims=True)
    g_heads[...] += jnp.where(tall == 0, g_decay, 0.0) + jnp.where(tall == 2, g_step, 0.0)

    b = act[:, DI : DI + NS].astype(BF16)
    c = act[:, DI + NS : DI + 2 * NS].astype(BF16)
    ds = d_scores[...].astype(BF16)
    d_val[:, DI : DI + NS] = dot(ds, c, ((0,), (0,)))
    d_val[:, DI + NS : DI + 2 * NS] = dot(ds, b)
    same = [meta[:, j : j + 1] for j in range(KC - 1)]

    @pl.loop(0, CONV // LANE)
    def _(k):
        x = proj[:, cols(k + DI // LANE)]
        tap = taps[:, cols(k)]
        dt = d_val[:, cols(k)] * d_act[:, cols(k)]
        g_taps[pl.ds(KC, 1), cols(k)] = jnp.sum(dt, axis=0, keepdims=True)
        g_taps[pl.ds(KC - 1, 1), cols(k)] = jnp.sum(dt * x, axis=0, keepdims=True)
        dc = dt * tap[KC - 1 : KC]
        for j in range(1, KC):
            ds_j = dt * same[j - 1]
            g_taps[pl.ds(KC - 1 - j, 1), cols(k)] = jnp.sum(
                ds_j * pltpu.roll(x, j, 0), axis=0, keepdims=True
            )
            dc = dc + pltpu.roll(ds_j, n - j, 0) * tap[KC - 1 - j : KC - j]
        d_proj_b[:, cols(k + DI // LANE)] = dc.astype(BF16)

    wide = 3 * LANE

    def add(k, total):
        return total + dot(d_proj_b[:, cols(k, wide)], w_in[:, cols(k, wide)], ((1,), (1,)))

    d_normed = lax.fori_loop(0, d_proj_b.shape[1] // wide, add, jnp.zeros((n, d), F32))
    g_gain[...] = jnp.sum(d_normed * h * root, axis=0, keepdims=True)
    u = d_normed * gain[...]
    back = jnp.sum(u * h, axis=-1, keepdims=True) * (root * root * root) / d
    grad_hidden[...] = upstream[...] + root * u - h * back


def per_device(
    hidden_in, cotangent, seq_ids, norm_gain, in_weight, conv_weight, conv_bias, out_gain,
    out_weight, decay_log, skip_gain, step_bias,
):
    n, d = hidden_in.shape
    rows, width = in_weight.shape
    padded = -(-width // LANE) * LANE
    spare = padded - width
    small = jnp.concatenate([norm_gain, conv_weight.reshape(-1), conv_bias, out_gain])
    packed = jnp.pad(small, (0, rows * spare - small.shape[0])).reshape(rows, spare)
    sent = jnp.concatenate([in_weight, packed], axis=1)
    w_in = lax.all_gather(sent, AXES, axis=0, tiled=True)
    w_out = lax.all_gather(out_weight, AXES, axis=0, tiled=True)
    devices = w_in.shape[0] // rows
    table = w_in[:, width:].reshape(devices, rows * spare).astype(F32)
    sizes = [norm_gain.shape[0]] + [conv_bias.shape[0]] * (KC + 1) + [out_gain.shape[0]]
    parts, at = [], 0
    for size in sizes:
        parts.append(table[:, at : at + size].reshape(1, -1))
        at += size
    gain = parts[0]
    taps = jnp.concatenate(parts[1 : KC + 2] + [jnp.zeros((8 - KC - 1, CONV), F32)])
    o_gain = parts[KC + 2]
    skip_e = jnp.repeat(skip_gain, HD)[None]
    heads = jnp.pad(jnp.stack([step_bias, -jnp.exp(decay_log)]), ((0, 6), (0, LANE - NH)))
    matched = [
        jnp.concatenate([jnp.zeros((j,), F32), (seq_ids[j:] == seq_ids[:-j]).astype(F32)])
        for j in range(1, KC)
    ]
    meta = jnp.stack(matched + [(seq_ids >= 0).astype(F32)], axis=1)
    seq_col, seq_row = seq_ids[:, None], seq_ids[None]
    limit = pltpu.CompilerParams(vmem_limit_bytes=56 * 1024 * 1024)

    saved = pl.pallas_call(
        forward_kernel,
        name="forward",
        out_shape=[
            sds(n, d, dtype=BF16), sds(n, padded), sds(n, CONV), sds(n, CONV), sds(n, DI),
            sds(n, DI, dtype=BF16), sds(n, DI), sds(n, LANE), sds(n, LANE), sds(n, DI),
            sds(n, DI), sds(LANE, n), sds(n, n),
        ],
        in_specs=[VM] * 10,
        out_specs=[VM] * 13,
        compiler_params=limit,
        cost_estimate=pl.CostEstimate(flops=4 * 10**9, bytes_accessed=10**7, transcendentals=10**6),
    )(hidden_in, w_in, gain, taps, o_gain, skip_e, heads, meta, seq_col, seq_row)
    normed_b, proj, act, d_act, inner, mixed_b, gated, stats, step, step_e, cum_e, cum_t, scores = saved
    rows_first = (((0,), (0,)), ((), ()))
    grad_out = lax.dot_general(
        mixed_b, cotangent.astype(BF16), rows_first, preferred_element_type=F32
    ).astype(BF16)
    own_out = lax.psum_scatter(grad_out, AXES, scatter_dimension=0, tiled=True)

    grad_hidden, d_proj_b, g_gain, g_taps, g_out, g_heads = pl.pallas_call(
        backward_kernel,
        name="backward",
        out_shape=[
            sds(n, d), sds(n, padded, dtype=BF16), sds(1, d), sds(8, CONV), sds(1, DI), sds(8, LANE),
        ],
        in_specs=[VM] * 23,
        out_specs=[VM] * 6,
        scratch_shapes=[
            pltpu.VMEM((n, CONV), F32), pltpu.VMEM((n, DI), F32), pltpu.VMEM((n, LANE), F32),
            pltpu.VMEM((n, n), F32),
        ],
        compiler_params=limit,
        cost_estimate=pl.CostEstimate(flops=8 * 10**9, bytes_accessed=10**7, transcendentals=10**6),
    )(
        hidden_in, cotangent, w_in, w_out, gain, taps, o_gain, skip_e, heads, meta, seq_col, seq_row,
        proj, act, d_act, inner, gated, stats, step, step_e, cum_e, cum_t, scores,
    )
    pieces = [g_gain] + [g_taps[j : j + 1] for j in range(KC + 1)] + [g_out]
    table = jnp.concatenate([p.reshape(devices, -1) for p in pieces], axis=1)
    table = jnp.pad(table, ((0, 0), (0, rows * spare - table.shape[1])))
    table = jnp.pad(table.reshape(devices * rows, spare), ((0, 0), (width, 0)))
    grad_in = lax.dot_general(normed_b, d_proj_b, rows_first, preferred_element_type=F32)
    own = lax.psum_scatter(
        (grad_in + table).astype(BF16), AXES, scatter_dimension=0, tiled=True
    ).astype(F32)
    block_out = hidden_in + jnp.dot(mixed_b, w_out, preferred_element_type=F32)
    head_sums = lax.psum(g_heads, AXES)
    tail = own[:, width:].reshape(-1)
    outs, at = [], 0
    for size in sizes:
        outs.append(tail[at : at + size])
        at += size
    return (
        block_out,
        grad_hidden,
        outs[0],
        own[:, :width],
        jnp.stack(outs[1 : KC + 1]),
        outs[KC + 1],
        outs[KC + 2],
        own_out.astype(F32),
        head_sums[0, :NH],
        head_sums[1, :NH],
        head_sums[2, :NH],
    )


def solution(mesh):
    rows, flat = P(AXES, None), P(AXES)
    return jax.shard_map(
        per_device,
        mesh=mesh,
        in_specs=(rows, rows, flat, flat, rows, P(None, AXES), flat, flat, rows, P(), P(), P()),
        out_specs=(rows, rows, flat, rows, P(None, AXES), flat, flat, rows, P(), P(), P()),
        check_vma=False,
    )
```

time: 553 us -> 363 us (0.66); the launches traced: 543 us -> 362 us
  blocking collectives: 165 us -> 38.8 us
  waiting for transfers between devices: 142 us -> 213 us
  matrix products: 76.4 us -> 11.7 us
  local copies, waits for them, and re-layouts: 77.4 us -> 14.3 us
  Pallas kernels: 0 us -> 56.7 us
  other arithmetic: 62.2 us -> 12.9 us
  between operations: 19.6 us -> 14 us
    unnamed x3 -> x0, blocking collectives: 86.9 us -> none
    all_gather x2, waiting for transfers between devices: 0.01 us -> 85.9 us  [the longest x1 59.4 us: per_device(): w_in = lax.all_gather(sent, AXES, axis=0, tiled=True)]
    dot_general x17 -> x3, matrix products: 74.9 us -> 11.7 us  [the longest x1 5.43 us: per_device(): lax.dot_general(normed_b, d_proj_b, rows_first, preferred_element_type=F32)]
    pallas_call x0 -> x2, Pallas kernels: none -> 56.7 us  [the longest x1 32.2 us: per_device(): pl.pallas_call(backward_kernel, name='backward', out_shape=[sds(n, d), sd...]
    all_gather x1 -> x0, blocking collectives: 40.9 us -> none  [per_device(): lax.all_gather(conv_weight, ('dp', 'fsdp'), axis=1, tiled=True)]
    reduce_scatter x3 -> x1, waiting for transfers between devices: 56.1 us -> 20.1 us  [per_device(): own_out = lax.psum_scatter(grad_out, AXES, scatter_dimension=0, tiled=True)]
    unnamed x9 -> x5, waiting for transfers between devices: 85.5 us -> 107 us
    reduce_sum x11 -> x0, other arithmetic: 21.2 us -> none  [the longest x1 6.37 us: mixer(): summed = conv_shift[None, :] + conv_in * conv_kernel[KC - 1][None, :]]
  transfers between devices with their start and end apart: 7 -> 4, of which waited for: 4 -> 4; matrix products, arithmetic and copies ran while one was open for 27% -> 8% of each run, Pallas kernels for 0% -> 16%
where the time goes in v1:
time: 363 us; the launch traced here: 362 us
  waiting for transfers between devices  213 us (59%)
  Pallas kernels  56.7 us (16%)
  blocking collectives  38.8 us (11%)
  local copies, waits for them, and re-layouts  14.3 us (4%)
  between operations  14 us (4%)
  other arithmetic  12.9 us (4%)
  matrix products  11.7 us (3%)
    unnamed x5, waiting for transfers between devices  107 us
    all_gather x1, waiting for transfers between devices, per_device(): w_in = lax.all_gather(sent, AXES, axis=0, tiled=True)  59.4 us
    psum x1, blocking collectives, per_device(): head_sums = lax.psum(g_heads, AXES)  38.8 us
    pallas_call x1, Pallas kernels, per_device(): pl.pallas_call(backward_kernel, name='backward', out_shape=[sds(n, d), sd...  32.2 us
    all_gather x1, waiting for transfers between devices, per_device(): w_out = lax.all_gather(out_weight, AXES, axis=0, tiled=True)  26.6 us
    pallas_call x1, Pallas kernels, per_device(): pl.pallas_call(forward_kernel, name='forward', out_shape=[sds(n, d, dtype...  24.5 us
    reduce_scatter x1, waiting for transfers between devices, per_device(): own_out = lax.psum_scatter(grad_out, AXES, scatter_dimension=0, tiled=True)  20.1 us
  transfers between devices with their start and end apart: 4, of which 4 were waited for; matrix products, arithmetic and copies ran while one was open for 8% of the time, Pallas kernels for 16%

profile of v1, /device:TPU:0, one launch (start us, length us, event | category | flops | bytes accessed | tf_op | source)
XLA Modules:
  0.0 361.9 jit_solution(3287179104776780474)
XLA Ops:
  7.2 0.8 reshape.79
  8.0 0.8 fusion.7
  8.8 0.1 reshape.80
  8.9 1.7 pad_maximum_fusion
  10.6 0.7 all-gather.5.cloned.1.call-update
  11.3 0.8 slice_compare_fusion.1
  12.2 0.1 concatenate.26
  12.3 0.8 slice_compare_fusion
  13.1 0.1 concatenate.27
  13.2 0.8 slice_compare_fusion.2
  14.0 0.1 pad_add_fusion.1
  14.1 0.7 broadcast_compare_fusion
  14.8 0.7 broadcast_in_dim.13
  15.5 0.7 broadcast_in_dim_reshape.3.skip_e
  16.2 0.2 copy.29
  16.4 0.7 stack.53.meta
  17.0 1.5 copy.30.seq_col
  18.5 0.7 negate_bitcast_fusion
  19.2 1.3 select_maximum_fusion.heads
  20.4 59.4 %all-gather.3.cloned.1.call-done.w_in = bf16[768,3456]{1,0:T(8,128)(2,1)} async-done(((bf16[24,3456]{1,0:T(8,128)(2,1)}), bf16[768,3456]{1,0:T(8,128)(2,1)}) %all-gather.3.cloned.1.call-update) | async-done | bytes 5308432 | tf_op jit(solution)/shard_map/all_gather | solution.py:263
  79.8 1.0 slice_convert_fusion
  80.9 0.2 reshape.97
  81.0 0.1 slice.131
  81.1 0.7 reshape.87.out_gain
  81.8 0.7 reshape.81.gain
  82.5 0.1 fusion.8
  82.6 0.1 reshape.86
  82.7 0.1 reshape.85
  82.7 0.1 reshape.84
  82.8 0.1 reshape.83
  82.9 0.1 reshape.82
  83.0 0.7 concatenate.24.taps
  83.7 24.5 %forward.1 = (bf16[256,768]{1,0:T(8,128)(2,1)}, f32[256,3456]{1,0:T(8,128)}, f32[256,1792]{1,0:T(8,128)}, f32[256,1792]{1,0:T(8,128)}, f32[256,1536]{1,0:T(8,128...) custom-call(f32[256,768]{1,0:T(8,128)} %hidden.3, ...), custom_call_target="tpu_custom_call" | custom-call | flops 4000000000 | bytes 10000000 | tf_op jit(solution)/shard_map/forward/pallas_call | solution.py:285
  108.2 3.5 convolution_convert_fusion
  111.7 0.0 reduce-scatter.7.cloned.1.call-start
  111.7 26.6 %all-gather.5.cloned.1.call-done.w_out = bf16[1536,768]{1,0:T(8,128)(2,1)} async-done(((bf16[48,768]{1,0:T(8,128)(2,1)}), bf16[1536,768]{1,0:T(8,128)(2,1)}) %all-gather.5.cloned.1.call-update) | async-done | bytes 2359312 | tf_op jit(solution)/shard_map/all_gather | solution.py:264
  138.3 32.2 %backward.1 = (f32[256,768]{1,0:T(8,128)}, bf16[256,3456]{1,0:T(8,128)(2,1)}, f32[1,768]{1,0:T(1,128)}, f32[8,1792]{1,0:T(8,128)}, f32[1,1536]{1,0:T(1,128)}, /*index=5*/f32[8,128]{1,0:T(8,128)}) custom-call(f32[256,768]{1,0:T(8,128)} %hidden.3, f32[256,768]{1,0:T(8,128)} %upstream.1, bf16[768,3456]{1,0:T(8,128)(2,1)} %all-gather.3.cloned.1.call-done.w_in, ...), custom_call_target="tpu_custom_call" | custom-call | flops 8000000000 | bytes 10000000 | tf_op jit(solution)/shard_map/backward/pallas_call | solution.py:305
  170.5 0.7 reduce
  171.2 0.7 reduce.6
  172.0 0.1 reshape.94
  172.0 0.1 reshape.88
  172.1 1.1 slice_reduce_fusion
  173.2 0.1 reshape.93
  173.3 0.1 reshape.92
  173.4 0.1 reshape.91
  173.5 0.1 reshape.90
  173.6 0.1 reshape.89
  173.7 0.1 concatenate.28
  173.8 0.2 reshape.95
  174.1 5.4 %add_convert_fusion = bf16[768,3456]{1,0:T(8,128)(2,1)} fusion(f32[768,104]{1,0:T(8,128)S(1)} %reshape.95, bf16[256,768]{1,0:T(8,128)(2,1)S(1)} %copy-done.4, bf16[256,3456]{1,0:T(8,128)(2,1)} %get-tuple-element.44), kind=kOutput, calls=%fused_computation | convolution fusion | flops 1364262912 | bytes 7790592 | tf_op jit(solution)/shard_map/dot_general | solution.py:327
  179.5 0.6 copy-done.3
  180.2 38.8 %psum.7 = f32[8,128]{1,0:T(8,128)S(1)} all-reduce(f32[8,128]{1,0:T(8,128)S(1)} %copy-done.3), channel_id=1, replica_groups=mesh['dp'=8,'fsdp'=4] {'dp','fsdp'}, use_global_device_ids=true, to_apply=%region_2.3 | all-reduce | flops 1024 | bytes 8192 | tf_op jit(solution)/shard_map/psum | solution.py:332
  219.0 0.5 slice_bitcast_fusion.4
  219.5 2.8 convolution_add_fusion
  222.3 20.1 %reduce-scatter.5.cloned.1.call-done = bf16[48,768]{1,0:T(8,128)(2,1)} async-done(((bf16[1536,768]{1,0:T(8,128)(2,1)}), bf16[48,768]{1,0:T(8,128)(2,1)}) %reduce-scatter.5.cloned.1.call-update) | async-done | bytes 73744 | tf_op jit(solution)/shard_map/reduce_scatter | solution.py:303
  242.4 1.6 convert_element_type.39
  244.0 106.6 %reduce-scatter.7.cloned.1.call-done = bf16[24,3456]{1,0:T(8,128)(2,1)} async-done(((bf16[768,3456]{1,0:T(8,128)(2,1)}), bf16[24,3456]{1,0:T(8,128)(2,1)}) %reduce-scatter.7.cloned.1.call-update) | async-done | bytes 165904
  350.5 0.8 slice.132
  351.3 0.1 reshape.96
  351.4 0.6 slice.140
  352.0 0.5 slice.133
  352.5 0.6 fusion.9
  353.1 0.6 pad_maximum_fusion.1
  353.7 1.7 slice.134
  (23 shorter events, 0.3 us)
Async XLA Ops:
  7.2 72.6 %all-gather.3.cloned.1.call-start = ((), (), s32[]{:S(2)}) async-start(), calls=%async_computation.2 | async-start | bytes 5474304 | tf_op jit(solution)/shard_map/all_gather | solution.py:263
  10.5 127.7 %all-gather.5.cloned.1.call-start = ((), (), s32[]{:S(2)}) async-start(), calls=%async_computation.3 | async-start | bytes 2433024 | tf_op jit(solution)/shard_map/all_gather | solution.py:264
  11.3 231.1 %reduce-scatter.5.cloned.1.call-start = ((), (), s32[]{:S(2)}) async-start(), calls=%async_computation.4 | async-start | bytes 2433024 | tf_op jit(solution)/shard_map/reduce_scatter | solution.py:303
  83.7 24.5 %copy-start.2 = (f32[256,768]{1,0:T(8,128)S(1)}, f32[256,768]{1,0:T(8,128)}, u32[]{:S(2)}) copy-start(f32[256,768]{1,0:T(8,128)} %upstream.1) | copy-start | bytes 2359300
  111.7 238.9 %reduce-scatter.7.cloned.1.call-start = ((), (), s32[]{:S(2)}) async-start(), calls=%async_computation.5 | async-start | bytes 5474304
  138.3 35.8 %copy-start.4 = (bf16[256,768]{1,0:T(8,128)(2,1)S(1)}, bf16[256,768]{1,0:T(8,128)(2,1)}, u32[]{:S(2)}) copy-start(bf16[256,768]{1,0:T(8,128)(2,1)} %get-tuple-element.43) | copy-start | bytes 1179652
  179.5 0.7 copy-start.3
  179.5 40.0 %copy-start = (bf16[256,1536]{1,0:T(8,128)(2,1)S(1)}, bf16[256,1536]{1,0:T(8,128)(2,1)}, u32[]{:S(2)}) copy-start(bf16[256,1536]{1,0:T(8,128)(2,1)} %get-tuple-element.30) | copy-start | bytes 2359300
  179.5 40.0 %copy-start.1 = (bf16[1536,768]{1,0:T(8,128)(2,1)S(1)}, bf16[1536,768]{1,0:T(8,128)(2,1)}, u32[]{:S(2)}) copy-start(bf16[1536,768]{1,0:T(8,128)(2,1)} %all-gather.5.cloned.1.call-done.w_out) | copy-start | bytes 7077892
Sparse Core Ops, SparseCore 0:
  11.5 68.2 all-gather.2
  82.7 55.5 all-gather.4
  143.6 98.7 reduce-scatter.4
  248.0 102.5 reduce-scatter.6

commit v2 on v1

--- a/solution.py
+++ b/solution.py
@@ -259,11 +259,16 @@
     spare = padded - width
     small = jnp.concatenate([norm_gain, conv_weight.reshape(-1), conv_bias, out_gain])
     packed = jnp.pad(small, (0, rows * spare - small.shape[0])).reshape(rows, spare)
-    sent = jnp.concatenate([in_weight, packed], axis=1)
+    folds = out_weight.shape[0] // rows
+    halves = [out_weight[j * rows : (j + 1) * rows] for j in range(folds)]
+    sent = jnp.concatenate([in_weight, packed] + halves, axis=1)
     w_in = lax.all_gather(sent, AXES, axis=0, tiled=True)
-    w_out = lax.all_gather(out_weight, AXES, axis=0, tiled=True)
     devices = w_in.shape[0] // rows
-    table = w_in[:, width:].reshape(devices, rows * spare).astype(F32)
+    w_out = jnp.stack(
+        [w_in[:, padded + j * d : padded + (j + 1) * d].reshape(devices, rows, d) for j in range(folds)],
+        axis=1,
+    ).reshape(-1, d)
+    table = w_in[:, width:padded].reshape(devices, rows * spare).astype(F32)
     sizes = [norm_gain.shape[0]] + [conv_bias.shape[0]] * (KC + 1) + [out_gain.shape[0]]
     parts, at = [], 0
     for size in sizes:
@@ -300,7 +305,6 @@
     grad_out = lax.dot_general(
         mixed_b, cotangent.astype(BF16), rows_first, preferred_element_type=F32
     ).astype(BF16)
-    own_out = lax.psum_scatter(grad_out, AXES, scatter_dimension=0, tiled=True)
 
     grad_hidden, d_proj_b, g_gain, g_taps, g_out, g_heads = pl.pallas_call(
         backward_kernel,
@@ -325,12 +329,18 @@
     table = jnp.pad(table, ((0, 0), (0, rows * spare - table.shape[1])))
     table = jnp.pad(table.reshape(devices * rows, spare), ((0, 0), (width, 0)))
     grad_in = lax.dot_general(normed_b, d_proj_b, rows_first, preferred_element_type=F32)
-    own = lax.psum_scatter(
-        (grad_in + table).astype(BF16), AXES, scatter_dimension=0, tiled=True
-    ).astype(F32)
+    split = grad_out.reshape(devices, folds, rows, d)
+    partial = jnp.concatenate(
+        [(grad_in + table).astype(BF16)] + [split[:, j].reshape(-1, d) for j in range(folds)], axis=1
+    )
+    partial, g_heads = lax.optimization_barrier((partial, g_heads))
+    own = lax.psum_scatter(partial, AXES, scatter_dimension=0, tiled=True).astype(F32)
+    own_out = jnp.concatenate(
+        [own[:, padded + j * d : padded + (j + 1) * d] for j in range(folds)], axis=0
+    )
     block_out = hidden_in + jnp.dot(mixed_b, w_out, preferred_element_type=F32)
     head_sums = lax.psum(g_heads, AXES)
-    tail = own[:, width:].reshape(-1)
+    tail = own[:, width:padded].reshape(-1)
     outs, at = [], 0
     for size in sizes:
         outs.append(tail[at : at + size])
@@ -343,7 +353,7 @@
         jnp.stack(outs[1 : KC + 1]),
         outs[KC + 1],
         outs[KC + 2],
-        own_out.astype(F32),
+        own_out,
         head_sums[0, :NH],
         head_sums[1, :NH],
         head_sums[2, :NH],

time: 363 us -> 292 us (0.80)
  waiting for transfers between devices: 213 us -> 138 us
  local copies, waits for them, and re-layouts: 14.3 us -> 20.9 us
  matrix products: 11.7 us -> 5.24 us
    unnamed x5 -> x3, waiting for transfers between devices: 107 us -> 70.1 us
    all_gather x1 -> x0, waiting for transfers between devices: 26.6 us -> none  [per_device(): w_out = lax.all_gather(out_weight, AXES, axis=0, tiled=True)]
    reduce_scatter x1 -> x0, waiting for transfers between devices: 20.1 us -> none  [per_device(): own_out = lax.psum_scatter(grad_out, AXES, scatter_dimension=0, tiled=True)]
    all_gather x1, waiting for transfers between devices: 59.4 us -> 68 us  [per_device(): w_in = lax.all_gather(sent, AXES, axis=0, tiled=True)]
    dot_general x1, matrix products: 5.43 us -> 1.62 us  [per_device(): lax.dot_general(normed_b, d_proj_b, rows_first, preferred_element_type=F32)]
  transfers between devices with their start and end apart: 4 -> 2, of which waited for: 4 -> 2; matrix products, arithmetic and copies ran while one was open for 8% -> 4% of each run, Pallas kernels for 16% -> 0%
where the time goes in v2:
time: 292 us; the launch traced here: 291 us
  waiting for transfers between devices  138 us (47%)
  Pallas kernels  57.8 us (20%)
  blocking collectives  39.2 us (13%)
  local copies, waits for them, and re-layouts  20.9 us (7%)
  other arithmetic  15.5 us (5%)
  between operations  14.3 us (5%)
  matrix products  5.24 us (2%)
    unnamed x3, waiting for transfers between devices  70.1 us
    all_gather x1, waiting for transfers between devices, per_device(): w_in = lax.all_gather(sent, AXES, axis=0, tiled=True)  68 us
    psum x1, blocking collectives, per_device(): head_sums = lax.psum(g_heads, AXES)  39.2 us
    pallas_call x1, Pallas kernels, per_device(): pl.pallas_call(backward_kernel, name='backward', out_shape=[sds(n, d), sd...  32.9 us
    pallas_call x1, Pallas kernels, per_device(): pl.pallas_call(forward_kernel, name='forward', out_shape=[sds(n, d, dtype...  24.9 us
  transfers between devices with their start and end apart: 2, of which 2 were waited for; matrix products, arithmetic and copies ran while one was open for 4% of the time, Pallas kernels for 0%

profile of v2, /device:TPU:0, one launch (start us, length us, event | category | flops | bytes accessed | tf_op | source)
XLA Modules:
  0.0 291.0 jit_solution(2465814118846375857)
XLA Ops:
  7.2 0.8 reshape.85
  8.0 0.8 fusion.7
  8.8 0.1 reshape.86
  8.9 0.8 fusion.12
  9.7 1.7 concatenate.29
  11.4 0.8 slice_compare_fusion.1
  12.2 0.1 concatenate.32
  12.3 0.8 slice_compare_fusion
  13.2 0.8 slice_compare_fusion.2
  14.1 0.1 pad_add_fusion.1
  14.2 0.7 broadcast_compare_fusion
  14.9 0.7 broadcast_in_dim.13
  15.6 0.7 broadcast_in_dim_reshape.3.skip_e
  16.3 0.2 copy.37
  16.4 0.7 stack.56.meta
  17.1 1.5 copy.38.seq_col
  18.6 0.7 negate_bitcast_fusion
  19.3 1.3 select_maximum_fusion.heads
  20.5 68.0 %all-gather.2.cloned.1.call-done.w_in = bf16[768,4992]{1,0:T(8,128)(2,1)} async-done(((bf16[24,4992]{1,0:T(8,128)(2,1)}), bf16[768,4992]{1,0:T(8,128)(2,1)}) %all-gather.2.cloned.1.call-update) | async-done | bytes 7667728 | tf_op jit(solution)/shard_map/all_gather | solution.py:265
  88.5 1.0 slice_convert_fusion
  89.6 0.2 reshape.105
  89.8 0.1 fusion.10
  89.9 0.7 reshape.93.out_gain
  90.6 0.7 reshape.87.gain
  91.2 0.1 reshape.92
  91.3 0.1 reshape.91
  91.4 0.1 reshape.90
  91.5 0.1 reshape.89
  91.6 0.1 reshape.88
  91.7 1.8 fusion.8
  93.5 1.7 pad_maximum_fusion.1
  95.2 0.7 concatenate.30.taps
  95.9 24.9 %forward.1 = (bf16[256,768]{1,0:T(8,128)(2,1)}, f32[256,3456]{1,0:T(8,128)}, f32[256,1792]{1,0:T(8,128)}, f32[256,1792]{1,0:T(8,128)}, f32[256,1536]{1,0:T(8,128...) custom-call(f32[256,768]{1,0:T(8,128)} %hidden.3, ...), custom_call_target="tpu_custom_call" | custom-call | flops 4000000000 | bytes 10000000 | tf_op jit(solution)/shard_map/forward/pallas_call | solution.py:290
  120.8 32.9 %backward.1 = (f32[256,768]{1,0:T(8,128)}, bf16[256,3456]{1,0:T(8,128)(2,1)}, f32[1,768]{1,0:T(1,128)}, f32[8,1792]{1,0:T(8,128)}, f32[1,1536]{1,0:T(1,128)}, /*index=5*/f32[8,128]{1,0:T(8,128)}) custom-call(f32[256,768]{1,0:T(8,128)} %hidden.3, f32[256,768]{1,0:T(8,128)} %upstream.1, bf16[768,4992]{1,0:T(8,128)(2,1)} %all-gather.2.cloned.1.call-done.w_in, ...), custom_call_target="tpu_custom_call" | custom-call | flops 8000000000 | bytes 10000000 | tf_op jit(solution)/shard_map/backward/pallas_call | solution.py:309
  153.7 0.7 reduce
  154.4 0.7 reduce.6
  155.2 0.1 reshape.95
  155.3 1.1 slice_reduce_fusion
  156.4 0.1 reshape.100
  156.5 0.1 reshape.99
  156.6 0.1 reshape.98
  156.6 0.1 reshape.97
  156.7 0.1 reshape.96
  156.8 0.1 concatenate.34
  156.9 0.2 reshape.102
  157.2 0.8 convolution_convert_fusion
  158.1 0.2 fusion.9
  158.2 1.3 copy-done.4
  159.6 1.6 add_convert_fusion
  161.2 3.5 %pad_maximum_fusion = bf16[768,4992]{1,0:T(8,128)(2,1)} fusion(bf16[768,768]{1,0:T(8,128)(2,1)S(1)} %bitcast.44, bf16[768,768]{1,0:T(8,128)(2,1)S(1)} %bitcast.43, bf16[768,3456]{1,0:T(8,128)(2,1)S(1)} %add_convert_fusion), kind=kLoop, calls=%fused_computation.1 | loop fusion | flops 23003136 | bytes 15335424 | tf_op jit(solution)/shard_map/concatenate | solution.py:333
  164.7 0.6 copy-done.3
  165.4 39.2 %psum.7 = f32[8,128]{1,0:T(8,128)S(1)} all-reduce(f32[8,128]{1,0:T(8,128)S(1)} %copy-done.3), channel_id=1, replica_groups=mesh['dp'=8,'fsdp'=4] {'dp','fsdp'}, use_global_device_ids=true, to_apply=%region_1.2 | all-reduce | flops 1024 | bytes 8192 | tf_op jit(solution)/shard_map/psum | solution.py:342
  204.5 0.5 slice_bitcast_fusion.4
  205.1 2.8 convolution_add_fusion
  207.8 70.1 %reduce-scatter.4.cloned.1.call-done = bf16[24,4992]{1,0:T(8,128)(2,1)} async-done(((bf16[768,4992]{1,0:T(8,128)(2,1)}), bf16[24,4992]{1,0:T(8,128)(2,1)}) %reduce-scatter.4.cloned.1.call-update) | async-done | bytes 239632
  277.9 0.8 slice.168
  278.7 0.1 reshape.104
  278.8 0.6 slice.176
  279.4 0.5 slice.169
  279.9 0.6 fusion.13
  280.5 0.8 fusion.11
  281.3 0.7 pad_maximum_fusion.2
  281.9 0.6 pad_maximum_fusion.3
  282.5 1.7 slice.170
  (25 shorter events, 0.5 us)
Async XLA Ops:
  7.2 81.3 %all-gather.2.cloned.1.call-start = ((), (), s32[]{:S(2)}) async-start(), calls=%async_computation.1 | async-start | bytes 7907328 | tf_op jit(solution)/shard_map/all_gather | solution.py:265
  11.4 266.5 %reduce-scatter.4.cloned.1.call-start = ((), (), s32[]{:S(2)}) async-start(), calls=%async_computation.2 | async-start | bytes 7907328
  120.8 36.4 %copy-start.1 = (bf16[256,1536]{1,0:T(8,128)(2,1)S(1)}, bf16[256,1536]{1,0:T(8,128)(2,1)}, u32[]{:S(2)}) copy-start(bf16[256,1536]{1,0:T(8,128)(2,1)} %get-tuple-element.32) | copy-start | bytes 2359300
  120.8 36.4 %copy-start.2 = (f32[256,768]{1,0:T(8,128)S(1)}, f32[256,768]{1,0:T(8,128)}, u32[]{:S(2)}) copy-start(f32[256,768]{1,0:T(8,128)} %upstream.1) | copy-start | bytes 2359300
  158.1 1.5 copy-start.4
  158.1 1.5 copy-start.5
  164.7 0.7 copy-start.3
  164.7 40.4 %copy-start = (bf16[32,2,24,768]{3,2,1,0:T(8,128)(2,1)S(1)}, bf16[32,2,24,768]{3,2,1,0:T(8,128)(2,1)}, u32[]{:S(2)}) copy-start(bf16[32,2,24,768]{3,2,1,0:T(8,128)(2,1)} %pad_maximum_fusion.1) | copy-start | bytes 7077892
Sparse Core Ops, SparseCore 0:
  11.5 76.9 all-gather.1
  164.8 113.0 reduce-scatter.3

commit v3 on v2

--- a/solution.py
+++ b/solution.py
@@ -247,6 +247,25 @@
     u = d_normed * gain[...]
     back = jnp.sum(u * h, axis=-1, keepdims=True) * (root * root * root) / d
     grad_hidden[...] = upstream[...] + root * u - h * back
+
+
+def whole_kernel(
+    hidden, upstream, w_in, w_out, gain, taps, out_gain, skip_e, heads, meta, seq_col, seq_row,
+    normed_b, mixed_b, grad_hidden, d_proj_b, g_gain, g_taps, g_out, g_heads,
+    proj, act, d_act, inner, gated, stats, step, step_e, cum_e, cum_t, scores,
+    d_val, d_gated, acc, d_scores,
+):
+    shared = (gain, taps, out_gain, skip_e, heads, meta, seq_col, seq_row)
+    forward_kernel(
+        hidden, w_in, *shared,
+        normed_b, proj, act, d_act, inner, mixed_b, gated, stats, step, step_e, cum_e, cum_t, scores,
+    )
+    backward_kernel(
+        hidden, upstream, w_in, w_out, *shared,
+        proj, act, d_act, inner, gated, stats, step, step_e, cum_e, cum_t, scores,
+        grad_hidden, d_proj_b, g_gain, g_taps, g_out, g_heads,
+        d_val, d_gated, acc, d_scores,
+    )
 
 
 def per_device(
@@ -287,43 +306,33 @@
     seq_col, seq_row = seq_ids[:, None], seq_ids[None]
     limit = pltpu.CompilerParams(vmem_limit_bytes=56 * 1024 * 1024)
 
-    saved = pl.pallas_call(
-        forward_kernel,
-        name="forward",
+    rows_first = (((0,), (0,)), ((), ()))
+    normed_b, mixed_b, grad_hidden, d_proj_b, g_gain, g_taps, g_out, g_heads = pl.pallas_call(
+        whole_kernel,
+        name="mixer",
         out_shape=[
-            sds(n, d, dtype=BF16), sds(n, padded), sds(n, CONV), sds(n, CONV), sds(n, DI),
-            sds(n, DI, dtype=BF16), sds(n, DI), sds(n, LANE), sds(n, LANE), sds(n, DI),
-            sds(n, DI), sds(LANE, n), sds(n, n),
+            sds(n, d, dtype=BF16), sds(n, DI, dtype=BF16), sds(n, d), sds(n, padded, dtype=BF16),
+            sds(1, d), sds(8, CONV), sds(1, DI), sds(8, LANE),
         ],
-        in_specs=[VM] * 10,
-        out_specs=[VM] * 13,
+        in_specs=[VM] * 12,
+        out_specs=[VM] * 8,
+        scratch_shapes=[
+            pltpu.VMEM(shape, F32)
+            for shape in (
+                (n, padded), (n, CONV), (n, CONV), (n, DI), (n, DI), (n, LANE), (n, LANE), (n, DI),
+                (n, DI), (LANE, n), (n, n), (n, CONV), (n, DI), (n, LANE), (n, n),
+            )
+        ],
         compiler_params=limit,
-        cost_estimate=pl.CostEstimate(flops=4 * 10**9, bytes_accessed=10**7, transcendentals=10**6),
-    )(hidden_in, w_in, gain, taps, o_gain, skip_e, heads, meta, seq_col, seq_row)
-    normed_b, proj, act, d_act, inner, mixed_b, gated, stats, step, step_e, cum_e, cum_t, scores = saved
-    rows_first = (((0,), (0,)), ((), ()))
+        cost_estimate=pl.CostEstimate(
+            flops=12 * 10**9, bytes_accessed=10**7, transcendentals=10**6
+        ),
+    )(
+        hidden_in, cotangent, w_in, w_out, gain, taps, o_gain, skip_e, heads, meta, seq_col, seq_row
+    )
     grad_out = lax.dot_general(
         mixed_b, cotangent.astype(BF16), rows_first, preferred_element_type=F32
     ).astype(BF16)
-
-    grad_hidden, d_proj_b, g_gain, g_taps, g_out, g_heads = pl.pallas_call(
-        backward_kernel,
-        name="backward",
-        out_shape=[
-            sds(n, d), sds(n, padded, dtype=BF16), sds(1, d), sds(8, CONV), sds(1, DI), sds(8, LANE),
-        ],
-        in_specs=[VM] * 23,
-        out_specs=[VM] * 6,
-        scratch_shapes=[
-            pltpu.VMEM((n, CONV), F32), pltpu.VMEM((n, DI), F32), pltpu.VMEM((n, LANE), F32),
-            pltpu.VMEM((n, n), F32),
-        ],
-        compiler_params=limit,
-        cost_estimate=pl.CostEstimate(flops=8 * 10**9, bytes_accessed=10**7, transcendentals=10**6),
-    )(
-        hidden_in, cotangent, w_in, w_out, gain, taps, o_gain, skip_e, heads, meta, seq_col, seq_row,
-        proj, act, d_act, inner, gated, stats, step, step_e, cum_e, cum_t, scores,
-    )
     pieces = [g_gain] + [g_taps[j : j + 1] for j in range(KC + 1)] + [g_out]
     table = jnp.concatenate([p.reshape(devices, -1) for p in pieces], axis=1)
     table = jnp.pad(table, ((0, 0), (0, rows * spare - table.shape[1])))

time: 292 us -> 280 us (0.959)
  Pallas kernels: 57.8 us -> 45.2 us
    pallas_call x2 -> x1, Pallas kernels: 57.8 us -> 45.2 us  [per_device(): pl.pallas_call(whole_kernel, name='mixer', out_shape=[sds(n, d, dtype=BF1...]
where the time goes in v3:
time: 280 us; the launch traced here: 279 us
  waiting for transfers between devices  138 us (49%)
  Pallas kernels  45.2 us (16%)
  blocking collectives  39.2 us (14%)
  local copies, waits for them, and re-layouts  21.5 us (8%)
  other arithmetic  14.8 us (5%)
  between operations  14.3 us (5%)
  matrix products  6.37 us (2%)
    unnamed x3, waiting for transfers between devices  70.1 us
    all_gather x1, waiting for transfers between devices, per_device(): w_in = lax.all_gather(sent, AXES, axis=0, tiled=True)  68.1 us
    pallas_call x1, Pallas kernels, per_device(): pl.pallas_call(whole_kernel, name='mixer', out_shape=[sds(n, d, dtype=BF1...  45.2 us
    psum x1, blocking collectives, per_device(): head_sums = lax.psum(g_heads, AXES)  39.2 us
  transfers between devices with their start and end apart: 2, of which 2 were waited for; matrix products, arithmetic and copies ran while one was open for 4% of the time, Pallas kernels for 0%

profile of v3, /device:TPU:0, one launch (start us, length us, event | category | flops | bytes accessed | tf_op | source)
XLA Modules:
  0.0 279.5 jit_solution(17651642780488329714)
XLA Ops:
  7.2 0.8 reshape.85
  8.0 0.8 fusion.7
  8.8 0.1 reshape.86
  8.9 0.8 fusion.12
  9.7 1.7 concatenate.29
  11.4 0.8 slice_compare_fusion.1
  12.2 0.1 concatenate.32
  12.3 0.8 slice_compare_fusion
  13.2 0.1 concatenate.33
  13.2 0.8 slice_compare_fusion.2
  14.1 0.1 pad_add_fusion
  14.2 0.7 broadcast_compare_fusion
  14.9 0.7 broadcast_in_dim.13
  15.6 0.7 broadcast_in_dim_reshape.3.skip_e
  16.3 0.8 copy.44.meta
  17.1 1.5 copy.45.seq_col
  18.5 0.7 negate_bitcast_fusion
  19.2 1.3 select_maximum_fusion.heads
  20.4 68.1 %all-gather.2.cloned.1.call-done.w_in = bf16[768,4992]{1,0:T(8,128)(2,1)} async-done(((bf16[24,4992]{1,0:T(8,128)(2,1)}), bf16[768,4992]{1,0:T(8,128)(2,1)}) %all-gather.2.cloned.1.call-update) | async-done | bytes 7667728 | tf_op jit(solution)/shard_map/all_gather | solution.py:284
  88.5 1.0 slice_convert_fusion
  89.6 0.2 reshape.105
  89.8 0.1 fusion.10
  89.9 0.7 reshape.94.out_gain
  90.6 0.7 reshape.88.gain
  91.3 0.1 reshape.93
  91.4 0.1 reshape.92
  91.4 0.1 reshape.91
  91.5 0.1 reshape.90
  91.6 0.1 reshape.89
  91.7 1.8 fusion.8
  93.5 1.7 pad_maximum_fusion.1
  95.2 0.7 concatenate.30.taps
  95.9 45.2 %mixer.1 = (bf16[256,768]{1,0:T(8,128)(2,1)}, bf16[256,1536]{1,0:T(8,128)(2,1)}, f32[256,768]{1,0:T(8,128)}, bf16[256,3456]{1,0:T(8,128)(2,1)}, f32[1,768]{1,0:T...) custom-call(f32[256,768]{1,0:T(8,128)} %hidden.1, f32[256,768]{1,0:T(8,128)} %upstream.1, ...), custom_call_target="tpu_custom_call" | custom-call | flops 12000000000 | bytes 10000000 | tf_op jit(solution)/shard_map/mixer/pallas_call | solution.py:310
  141.1 0.7 reduce
  141.8 0.7 reduce.6
  142.5 0.1 reshape.101
  142.6 0.1 reshape.95
  142.6 1.1 slice_reduce_fusion
  143.8 0.1 reshape.100
  143.8 0.1 reshape.99
  143.9 0.1 reshape.98
  144.0 0.1 reshape.97
  144.1 0.1 reshape.96
  144.2 0.1 concatenate.34
  144.3 0.2 reshape.102
  144.6 2.0 convolution_convert_fusion
  146.6 0.2 fusion.9
  146.7 1.3 copy-done.4
  148.1 1.6 add_convert_fusion
  149.7 3.5 %pad_maximum_fusion = bf16[768,4992]{1,0:T(8,128)(2,1)} fusion(bf16[768,768]{1,0:T(8,128)(2,1)S(1)} %bitcast.44, bf16[768,768]{1,0:T(8,128)(2,1)S(1)} %bitcast.43, bf16[768,3456]{1,0:T(8,128)(2,1)S(1)} %add_convert_fusion), kind=kLoop, calls=%fused_computation.1 | loop fusion | flops 23003136 | bytes 15335424 | tf_op jit(solution)/shard_map/concatenate | solution.py:342
  153.2 0.7 copy-done.3
  153.9 39.2 %psum.7 = f32[8,128]{1,0:T(8,128)S(1)} all-reduce(f32[8,128]{1,0:T(8,128)S(1)} %copy-done.3), channel_id=1, replica_groups=mesh['dp'=8,'fsdp'=4] {'dp','fsdp'}, use_global_device_ids=true, to_apply=%region_1.2 | all-reduce | flops 1024 | bytes 8192 | tf_op jit(solution)/shard_map/psum | solution.py:351
  193.0 0.5 slice_bitcast_fusion.4
  193.6 2.8 convolution_add_fusion
  196.4 70.0 %reduce-scatter.4.cloned.1.call-done = bf16[24,4992]{1,0:T(8,128)(2,1)} async-done(((bf16[768,4992]{1,0:T(8,128)(2,1)}), bf16[24,4992]{1,0:T(8,128)(2,1)}) %reduce-scatter.4.cloned.1.call-update) | async-done | bytes 239632
  266.4 0.8 slice.168
  267.2 0.1 reshape.104
  267.2 0.6 slice.176
  267.8 0.5 slice.169
  268.3 0.6 fusion.13
  268.9 0.8 fusion.11
  269.7 0.7 pad_maximum_fusion.2
  270.4 0.6 pad_maximum_fusion.3
  271.0 1.7 slice.170
  (23 shorter events, 0.3 us)
Async XLA Ops:
  7.2 81.3 %all-gather.2.cloned.1.call-start = ((), (), s32[]{:S(2)}) async-start(), calls=%async_computation.1 | async-start | bytes 7907328 | tf_op jit(solution)/shard_map/all_gather | solution.py:284
  11.4 255.0 %reduce-scatter.4.cloned.1.call-start = ((), (), s32[]{:S(2)}) async-start(), calls=%async_computation.2 | async-start | bytes 7907328
  95.9 48.7 %copy-start.2 = (f32[256,768]{1,0:T(8,128)S(1)}, f32[256,768]{1,0:T(8,128)}, u32[]{:S(2)}) copy-start(f32[256,768]{1,0:T(8,128)} %upstream.1) | copy-start | bytes 2359300
  146.6 1.5 copy-start.4
  146.6 1.5 copy-start.5
  153.2 0.7 copy-start.3
  153.2 40.4 %copy-start = (bf16[32,2,24,768]{3,2,1,0:T(8,128)(2,1)S(1)}, bf16[32,2,24,768]{3,2,1,0:T(8,128)(2,1)}, u32[]{:S(2)}) copy-start(bf16[32,2,24,768]{3,2,1,0:T(8,128)(2,1)} %pad_maximum_fusion.1) | copy-start | bytes 7077892
  153.2 40.4 %copy-start.1 = (bf16[256,1536]{1,0:T(8,128)(2,1)S(1)}, bf16[256,1536]{1,0:T(8,128)(2,1)}, u32[]{:S(2)}) copy-start(bf16[256,1536]{1,0:T(8,128)(2,1)} %get-tuple-element.21) | copy-start | bytes 2359300
Sparse Core Ops, SparseCore 0:
  11.5 76.9 all-gather.1
  153.3 112.9 reduce-scatter.3
